TPU v7x, 512 devices: a whole 4x8x8 slice. The times are simulated.
512 devices in a mesh: segment: 32 (over y_lo, z), dp: 8 (over x, core), seq: 2 (over y_hi).
Axes of the slice: x: 4, y: 8 (y_hi: 2, y_lo: 4; y = y_hi * 4 + y_lo), z: 8, core: 2. Of those that a mesh axis runs over, the one named last changes fastest.
Arguments:
- stored_part_activation: bfloat16 [32, 2, 8, 256, 2048], P('segment', None, 'dp', 'seq'), may hold values from -64 to 64
- pending_sensitivity: bfloat16 [32, 8, 256, 2048], P('segment', 'dp', 'seq'), may hold values from -0.119628906 to 0.119628906
- uppermost_result_derivative: bfloat16 [1, 8, 256, 2048], P(None, 'dp', 'seq'), may hold values from -0.119628906 to 0.119628906
- scaling_factors: float32 [32, 4, 2048], P('segment'), may hold values from -0.5 to 5
- attended_tile_table: int32 [32, 2, 8, 2, 2], P('segment', None, 'dp'), may hold values from 0 to 1, as said below
- active_tile_number: int32 [32, 2, 8, 2], P('segment', None, 'dp'), may hold values from 1 to 2
Outputs:
- factor_derivatives: float32 [32, 4, 2048], P('segment')
Inputs may be any that keep to these rules, and one draw needn't show every extreme that they name: `attended_tile_table`: each list names every key block of its sample once; the allowed ones come first.
All inputs are finite; a program needn't handle non-finite values.
Results may differ from a plain program's by a relative error of at most 0.009.
Values may be sent and summed in bfloat16 or wider, within the bound.
A program may use at most 64 MiB of HBM per device.

v0:
```python
import jax
import jax.numpy as jnp
from jax import lax
from jax.sharding import PartitionSpec as P

HEAD_DIM = 128
BLK = 128
epsilon = 1e-06


def partner(block, axis, apart):
    count = lax.axis_size(axis)
    route = []
    for low in range(count):
        high = low | 1 << apart
        if high != low and high < count:
            route += [(low, high), (high, low)]
    return lax.ppermute(block, axis, route)


def from_behind(block, axis, distance):
    devices = range(lax.axis_size(axis))
    route = [(i - distance, i) for i in devices if i - distance in devices]
    return lax.ppermute(block, axis, route)


def normed_of(inputs):
    widened = inputs.astype(jnp.float32).reshape(
        inputs.shape[:-1] + (inputs.shape[-1] // HEAD_DIM, HEAD_DIM)
    )
    inv_rms = lax.rsqrt(jnp.mean(widened * widened, axis=-1, keepdims=True) + epsilon)
    return (widened * inv_rms, inv_rms)


def norm_back(grad_norm, norm_val, inv_rms):
    return inv_rms * (grad_norm - norm_val * jnp.mean(grad_norm * norm_val, axis=-1, keepdims=True))


def allowed_blocks(block_list, live_count):
    block_total = block_list.shape[0]
    live_slots = jnp.arange(block_total)[None, :] < live_count[:, None]
    matches = (block_list[:, :, None] == jnp.arange(block_total)[None, None, :]) & live_slots[
        :, :, None
    ]
    return jnp.any(matches, axis=1)


def token_mask(permitted, query_half, seq_index, dev_blocks):
    local_blocks = jnp.arange(dev_blocks, dtype=jnp.int32)
    query_rows = query_half * dev_blocks + local_blocks
    key_order = jnp.concatenate(
        [seq_index * dev_blocks + local_blocks, (1 - seq_index) * dev_blocks + local_blocks]
    )
    picked = permitted[query_rows[:, None], key_order[None, :]]
    return jnp.repeat(jnp.repeat(picked, BLK, axis=0), BLK, axis=1)


def attend(query_norm, key_norm, gain_heads, allowed, incoming, scaling):
    queries = (query_norm * gain_heads[0]).astype(jnp.bfloat16)
    key_mat = (key_norm * gain_heads[1]).astype(jnp.bfloat16)
    val_mat = (key_norm * gain_heads[2]).astype(jnp.bfloat16)
    scores = (
        jnp.einsum("thd,shd->hts", queries, key_mat, preferred_element_type=jnp.float32) * scaling
    )
    scores = jnp.where(allowed[None], scores, -jnp.inf)
    exped = jnp.exp(scores - jnp.max(scores, axis=-1, keepdims=True))
    probs = exped / jnp.sum(exped, axis=-1, keepdims=True)
    probs_low = probs.astype(jnp.bfloat16)
    output = jnp.einsum("hts,shd->thd", probs_low, val_mat, preferred_element_type=jnp.float32)
    grad_out = (gain_heads[3] * incoming).astype(jnp.bfloat16)
    grad_probs = jnp.einsum("thd,shd->hts", grad_out, val_mat, preferred_element_type=jnp.float32)
    grad_scores = (
        probs * (grad_probs - jnp.sum(probs * grad_probs, axis=-1, keepdims=True))
    ).astype(jnp.bfloat16)
    return (queries, key_mat, probs_low, output, grad_out, grad_scores)


def shards(
    stored_part_activation,
    pending_sensitivity,
    uppermost_result_derivative,
    scaling_factors,
    attended_tile_table,
    active_tile_number,
):
    segments = lax.axis_size("segment")
    segment_index = lax.axis_index("segment")
    seq_index = lax.axis_index("seq")
    window = stored_part_activation.shape[1]
    row_count = stored_part_activation.shape[3]
    channels = stored_part_activation.shape[4]
    head_count = channels // HEAD_DIM
    dev_blocks = row_count // BLK
    scaling = HEAD_DIM ** (-0.5)
    own_window = stored_part_activation[0, :, 0]
    gain_heads = scaling_factors[0].reshape(4, head_count, HEAD_DIM)
    incoming_sensitivity = pending_sensitivity[0, 0].astype(jnp.float32)
    totals = jnp.zeros((4, head_count, HEAD_DIM), jnp.float32)
    for step_index in range(window):
        own_rows = own_window[step_index]
        other_rows = partner(own_rows, "seq", 0)
        permitted = allowed_blocks(
            attended_tile_table[0, step_index, 0], active_tile_number[0, step_index, 0]
        )
        own_norm, own_inv = normed_of(own_rows)
        other_norm, other_inv = normed_of(other_rows)
        key_norm = jnp.concatenate([own_norm, other_norm], axis=0)
        incoming = incoming_sensitivity.reshape(row_count, head_count, HEAD_DIM)
        own_allowed = token_mask(permitted, seq_index, seq_index, dev_blocks)
        queries, key_mat, probs_low, output, grad_out, grad_scores = attend(
            own_norm, key_norm, gain_heads, own_allowed, incoming, scaling
        )
        grad_query = (
            jnp.einsum("hts,shd->thd", grad_scores, key_mat, preferred_element_type=jnp.float32)
            * scaling
        )
        grad_key = (
            jnp.einsum("hts,thd->shd", grad_scores, queries, preferred_element_type=jnp.float32)
            * scaling
        )
        grad_value = jnp.einsum(
            "hts,thd->shd", probs_low, grad_out, preferred_element_type=jnp.float32
        )
        key_part = grad_key * gain_heads[1] + grad_value * gain_heads[2]
        self_part = key_part[:row_count]
        key_terms = jnp.sum(grad_key * key_norm, axis=0)
        value_terms = jnp.sum(grad_value * key_norm, axis=0)
        if step_index < window - 1:
            lent = norm_back(key_part[row_count:], other_norm, other_inv).astype(jnp.bfloat16)
            returned = partner(lent, "seq", 0).astype(jnp.float32)
        grad_terms = jnp.stack(
            [
                jnp.sum(grad_query * own_norm, axis=0),
                key_terms,
                value_terms,
                jnp.sum(output * incoming, axis=0),
            ]
        )
        totals = totals + grad_terms
        if step_index < window - 1:
            grad_input = (
                incoming
                + norm_back(grad_query * gain_heads[0] + self_part, own_norm, own_inv)
                + returned
            )
            received = from_behind(grad_input.reshape(row_count, channels), "segment", -1)
            incoming_sensitivity = jnp.where(
                segment_index == segments - 1,
                uppermost_result_derivative[step_index, 0].astype(jnp.float32),
                received,
            )
    summed = lax.psum(totals.reshape(4, channels), ("dp", "seq"))
    return summed[None]


def solution(mesh):
    placed = (
        P("segment", None, "dp", "seq", None),
        P("segment", "dp", "seq", None),
        P(None, "dp", "seq", None),
        P("segment", None, None),
        P("segment", None, "dp", None, None),
        P("segment", None, "dp", None),
    )
    return jax.shard_map(
        shards, mesh=mesh, in_specs=placed, out_specs=P("segment", None, None), check_vma=False
    )
```

profile of v0, /device:TPU:24, one launch (start us, length us, event | category | flops | bytes accessed | tf_op | source)
XLA Modules:
  0.0 220.2 jit_solution(2187491883206557950)
XLA Ops:
  0.0 2.7 %slice_convert_fusion = (f32[1,1,1,128,2048]{4,3,2,1,0:T(8,128)}, bf16[128,2048]{1,0:T(8,128)(2,1)}, bf16[128,2048]{1,0:T(8,128)(2,1)}, f32[1,1,1,128,2048]{4,3,2,1,0:T(8,128)S(1)}) fusion(bf16[1,2,1,128,2048]{4,3,2,1,0:T(8,128)(2,1)} %param.6), kind=kLoop, calls=%fused_computation.75 | loop fusion | flops 524288 | bytes 4194304 | tf_op jit(solution)/shard_map/convert_element_type | solution.py:28
  2.7 5.0 %collective-permute-start = (bf16[128,2048]{1,0:T(8,128)(2,1)}, bf16[128,2048]{1,0:T(8,128)(2,1)}, u32[]{:S(2)}, u32[]{:S(2)}) collective-permute-start(bf16[128,2048]{1,0:T(8,128)(2,1)} %get-tuple-element.12), channel_id=1, source_target_pairs={{0,1},{1,0},{2,3},{3,2},{4,5},{5,4},{6,7},{7,6},{8,9},{9,8},{10,11... | collective-permute-start | bytes 1572872 | tf_op jit(solution)/shard_map/ppermute | solution.py:18
  7.8 4.7 %collective-permute-start.1 = (bf16[128,2048]{1,0:T(8,128)(2,1)}, bf16[128,2048]{1,0:T(8,128)(2,1)}, u32[]{:S(2)}, u32[]{:S(2)}) collective-permute-start(bf16[128,2048]{1,0:T(8,128)(2,1)} %get-tuple-element.13), channel_id=1, source_target_pairs={{0,1},{1,0},{2,3},{3,2},{4,5},{5,4},{6,7},{7,6},{8,9},{9,8},{10,11... | collective-permute-start | bytes 1572872 | tf_op jit(solution)/shard_map/ppermute | solution.py:18
  12.6 0.2 or_reduce_fusion
  12.9 0.1 and_reduce_fusion.1
  13.0 0.6 gather_fusion
  13.7 0.3 copy.49
  14.1 0.1 broadcast_multiply_fusion.3
  14.2 0.6 copy-done.11
  14.8 1.5 copy.58
  16.4 0.1 multiply_reduce_fusion.5
  16.5 0.1 and_reduce_fusion
  16.6 2.3 %copy.53 = f32[1,1,128,2048]{2,3,1,0:T(8,128)} copy(bf16[1,1,128,2048]{3,2,1,0:T(8,128)(2,1)} %param.7) | data formatting | bytes 1572864 | tf_op jit(solution)/shard_map/convert_element_type | solution.py:97
  18.9 0.6 gather_fusion.1
  19.5 1.1 broadcast_multiply_fusion.1
  20.6 12.6 %collective-permute-done = bf16[128,2048]{1,0:T(8,128)(2,1)} collective-permute-done((bf16[128,2048]{1,0:T(8,128)(2,1)}, bf16[128,2048]{1,0:T(8,128)(2,1)}, u32[]{:S(2)}, u32[]{:S(2)}) %collective-permute-start) | collective-permute-done | bytes 524320 | tf_op jit(solution)/shard_map/ppermute | solution.py:18
  33.2 1.2 copy.50
  34.5 1.1 broadcast_multiply_fusion.2
  35.6 3.9 %fusion.49 = (f32[16,128]{1,0:T(8,128)S(1)}, f32[16,128,256]{2,1,0:T(8,128)}) fusion(pred[256]{0:T(512)(128)(4,1)S(1)} %broadcast_bitcast_fusion.1, f32[16,128]{1,0:T(8,128)S(1)} %bitcast.124, f32[128,16,128]{0,2,1:T(8,128)} %broadcast_multiply_fusion.2, f32[128,16,128]{0,2,1:T(8,128)S(1)} %broadcast_multiply_fusion.3, f32[16,128]{1,0:T(8,128)S(1)} %bitcast.119), kind=kOutput, calls=%fused_computation.119 | convolution fusion | flops 138412288 | bytes 4219136 | tf_op jit(solution)/shard_map/sub | solution.py:66
  39.5 2.8 %fusion.26 = f32[16,128,256]{2,1,0:T(8,128)S(1)} fusion(f32[128,16,128]{0,2,1:T(8,128)} %bitcast.110, f32[16,128]{1,0:T(8,128)S(1)} %bitcast.141, f32[16,128,256]{2,1,0:T(8,128)} %get-tuple-element.24, f32[16,128]{1,0:T(8,128)S(1)} %get-tuple-element.23), kind=kOutput, calls=%fused_computation.70 | convolution fusion | flops 135790592 | bytes 5259264 | tf_op jit(solution)/shard_map/hts,thd->shd/dot_general | solution.py:121
  42.4 0.3 copy-done.5
  42.7 2.2 multiply_reduce_fusion.1
  44.9 0.7 multiply_convert_fusion.3
  45.6 1.9 fusion.5
  47.6 1.9 multiply_reduce_fusion.3
  49.5 1.0 multiply_convert_fusion.7
  50.5 6.3 %collective-permute-start.2 = (bf16[128,16,128]{0,2,1:T(8,128)(2,1)}, bf16[128,16,128]{0,2,1:T(8,128)(2,1)}, u32[]{:S(2)}, u32[]{:S(2)}) collective-permute-start(bf16[128,16,128]{0,2,1:T(8,128)(2,1)} %multiply_convert_fusion.7), channel_id=1, source_target_pairs={{0,1},{1,0},{2,3},{3,2},{4,5},{5,4},{6,7},{7,6},{8,9},{9,8},{10,11... | collective-permute-start | bytes 1572872 | tf_op jit(solution)/shard_map/ppermute | solution.py:18
  56.9 1.2 copy.59
  58.2 22.9 %collective-permute-done.2 = bf16[128,16,128]{0,2,1:T(8,128)(2,1)} collective-permute-done((bf16[128,16,128]{0,2,1:T(8,128)(2,1)}, bf16[128,16,128]{0,2,1:T(8,128)(2,1)}, u32[]{:S(2)}, u32[]{:S(2)}) %collective-permute-start.2) | collective-permute-done | bytes 524320 | tf_op jit(solution)/shard_map/ppermute | solution.py:18
  81.1 3.6 %convert_add_fusion = f32[128,16,128]{0,2,1:T(8,128)} fusion(bf16[128,16,128]{0,2,1:T(8,128)(2,1)} %collective-permute-done.2, f32[128,16,128]{0,2,1:T(8,128)} %bitcast.111, f32[128,16]{0,1:T(8,128)S(1)} %broadcast_multiply_fusion.7, f32[128,16]{0,1:T(8,128)S(1)} %add_rsqrt_fusion.3, f32[256,16,128]{0,2,1:T(8,128)} %copy-done.2, ...), kind=kLoop, calls=%fused_computation.45 | loop fusion | flops 2359296 | bytes 5791744 | tf_op jit(solution)/shard_map/add | solution.py:142
  84.7 2.6 %copy.62 = f32[128,2048]{1,0:T(8,128)} copy(f32[128,2048]{0,1:T(8,128)} %bitcast.114) | data formatting | bytes 2097152 | tf_op jit(solution)/shard_map/reshape | solution.py:146
  87.3 11.7 %collective-permute-start.3 = (f32[128,2048]{1,0:T(8,128)}, f32[128,2048]{1,0:T(8,128)}, u32[]{:S(2)}, u32[]{:S(2)}) collective-permute-start(f32[128,2048]{1,0:T(8,128)} %copy.62), channel_id=1, source_target_pairs={{16,0},{32,16},{48,32},{64,48},{80,64},{96,80},{112,96},{128,112},... | collective-permute-start | bytes 3145736 | tf_op jit(solution)/shard_map/ppermute | solution.py:24
  99.0 1.1 broadcast_multiply_fusion
  100.1 4.8 %fusion.50 = (f32[16,128]{1,0:T(8,128)S(1)}, f32[16,128,256]{2,1,0:T(8,128)}) fusion(pred[256]{0:T(512)(128)(4,1)S(1)} %broadcast_bitcast_fusion, f32[16,128]{1,0:T(8,128)S(1)} %bitcast.126, f32[128,16,128]{0,2,1:T(8,128)} %broadcast_multiply_fusion, f32[128,16,128]{0,2,1:T(8,128)} %broadcast_multiply_fusion.1, f32[16,128]{1,0:T(8,128)S(1)} %bitcast.121), kind=kOutput, calls=%fused_computation.120 | convolution fusion | flops 138412288 | bytes 4219136 | tf_op jit(solution)/shard_map/sub | solution.py:66
  104.9 2.6 %fusion.12 = f32[16,128]{1,0:T(8,128)S(1)} fusion(f32[128,16,128]{0,2,1:T(8,128)S(1)} %bitcast.113, f32[16,128]{1,0:T(8,128)S(1)} %bitcast.133, f32[128,16,128]{0,2,1:T(8,128)S(1)} %copy-done.1, f32[128,16,128]{0,2,1:T(8,128)S(1)} %broadcast_multiply_fusion.3, f32[16,128,256]{2,1,0:T(8,128)} %get-tuple-element.24, f32[16,128]{1,0:T(8,128)S(1)} %get-tuple-element.23), kind=kOutput, calls=%fused_computation.37 | convolution fusion | flops 137361408 | bytes 5267456 | tf_op jit(solution)/shard_map/hts,shd->thd/dot_general | solution.py:69
  107.5 14.2 %collective-permute-done.3 = f32[128,2048]{1,0:T(8,128)} collective-permute-done((f32[128,2048]{1,0:T(8,128)}, f32[128,2048]{1,0:T(8,128)}, u32[]{:S(2)}, u32[]{:S(2)}) %collective-permute-start.3) | collective-permute-done | bytes 1048608 | tf_op jit(solution)/shard_map/ppermute | solution.py:24
  121.7 1.3 convert_select_fusion
  123.1 1.3 copy.63
  124.4 3.4 %multiply_reduce_fusion = (f32[16,128]{1,0:T(8,128)S(1)}, f32[16,128,256]{2,1,0:T(8,128)S(1)}) fusion(f32[16,128,256]{2,1,0:T(8,128)S(1)} %copy-done.6, f32[16,128]{1,0:T(8,128)S(1)} %get-tuple-element.28, f32[16,128]{1,0:T(8,128)S(1)} %bitcast.134, f32[128,16,128]{0,2,1:T(8,128)} %broadcast_multiply_fusion, f32[128,16,128]{0,2,1:T(8,128)} %broadcast_multiply_fusion.1, ...), kind=kOutput, calls=%fused_computation.17 | convolution fusion | flops 137885696 | bytes 7372800 | tf_op jit(solution)/shard_map/thd,shd->hts/dot_general | solution.py:71
  127.8 0.8 multiply_convert_fusion
  128.6 0.4 copy-done.7
  129.0 0.3 copy-done.8
  129.4 0.7 fusion.13
  130.0 0.7 fusion.3
  130.7 0.5 copy-done.9
  131.3 1.1 fusion.2
  132.4 1.2 fusion.14
  133.7 86.5 %psum.7 = f32[1,4,2048]{2,1,0:T(4,128)} all-reduce(f32[1,4,2048]{2,1,0:T(4,128)S(1)} %fusion.32), channel_id=1, replica_groups=mesh['segment'=32,'dp'=8,'seq'=2] {'dp','seq'}, use_global_device_ids=true, to_apply=%region_22.23 | all-reduce | flops 8192 | bytes 65536 | tf_op jit(solution)/shard_map/psum | solution.py:152
  (44 shorter events, 0.8 us)
Async XLA Ops:
  0.0 12.8 %copy-start.13 = (s32[1,2,1,2]{3,2,1,0:T(1,128)S(1)}, s32[1,2,1,2]{3,2,1,0:T(1,128)}, u32[]{:S(2)}) copy-start(s32[1,2,1,2]{3,2,1,0:T(1,128)} %param.11) | copy-start | bytes 52
  0.0 12.8 %copy-start.12 = (s32[1,2,1,2,2]{4,3,2,1,0:T(2,128)S(1)}, s32[1,2,1,2,2]{4,3,2,1,0:T(2,128)}, u32[]{:S(2)}) copy-start(s32[1,2,1,2,2]{4,3,2,1,0:T(2,128)} %param.10) | copy-start | bytes 100
  2.7 30.5 %collective-permute-start = (bf16[128,2048]{1,0:T(8,128)(2,1)}, bf16[128,2048]{1,0:T(8,128)(2,1)}, u32[]{:S(2)}, u32[]{:S(2)}) collective-permute-start(bf16[128,2048]{1,0:T(8,128)(2,1)} %get-tuple-element.12), channel_id=1, source_target_pairs={{0,1},{1,0},{2,3},{3,2},{4,5},{5,4},{6,7},{7,6},{8,9},{9,8},{10,11... | collective-permute-start | bytes 1572872 | tf_op jit(solution)/shard_map/ppermute | solution.py:18
  7.8 49.1 %collective-permute-start.1 = (bf16[128,2048]{1,0:T(8,128)(2,1)}, bf16[128,2048]{1,0:T(8,128)(2,1)}, u32[]{:S(2)}, u32[]{:S(2)}) collective-permute-start(bf16[128,2048]{1,0:T(8,128)(2,1)} %get-tuple-element.13), channel_id=1, source_target_pairs={{0,1},{1,0},{2,3},{3,2},{4,5},{5,4},{6,7},{7,6},{8,9},{9,8},{10,11... | collective-permute-start | bytes 1572872 | tf_op jit(solution)/shard_map/ppermute | solution.py:18
  14.0 0.8 copy-start.11
  39.5 2.9 %copy-start = (f32[128,16,128]{0,2,1:T(8,128)S(1)}, f32[128,16,128]{0,2,1:T(8,128)}, u32[]{:S(2)}) copy-start(f32[128,16,128]{0,2,1:T(8,128)} %broadcast_multiply_fusion.2) | copy-start | bytes 3145732
  39.5 2.9 %copy-start.3 = (f32[1,1,128,2048]{2,3,1,0:T(8,128)S(1)}, f32[1,1,128,2048]{2,3,1,0:T(8,128)}, u32[]{:S(2)}) copy-start(f32[1,1,128,2048]{2,3,1,0:T(8,128)} %copy.53) | copy-start | bytes 3145732
  39.5 3.2 %copy-start.5 = (f32[16,128,256]{2,1,0:T(8,128)S(1)}, f32[16,128,256]{2,1,0:T(8,128)}, u32[]{:S(2)}) copy-start(f32[16,128,256]{2,1,0:T(8,128)} %get-tuple-element.24) | copy-start | bytes 6291460
  47.6 1.9 copy-start.2
  50.5 30.6 %collective-permute-start.2 = (bf16[128,16,128]{0,2,1:T(8,128)(2,1)}, bf16[128,16,128]{0,2,1:T(8,128)(2,1)}, u32[]{:S(2)}, u32[]{:S(2)}) collective-permute-start(bf16[128,16,128]{0,2,1:T(8,128)(2,1)} %multiply_convert_fusion.7), channel_id=1, source_target_pairs={{0,1},{1,0},{2,3},{3,2},{4,5},{5,4},{6,7},{7,6},{8,9},{9,8},{10,11... | collective-permute-start | bytes 1572872 | tf_op jit(solution)/shard_map/ppermute | solution.py:18
  87.3 34.4 %collective-permute-start.3 = (f32[128,2048]{1,0:T(8,128)}, f32[128,2048]{1,0:T(8,128)}, u32[]{:S(2)}, u32[]{:S(2)}) collective-permute-start(f32[128,2048]{1,0:T(8,128)} %copy.62), channel_id=1, source_target_pairs={{16,0},{32,16},{48,32},{64,48},{80,64},{96,80},{112,96},{128,112},... | collective-permute-start | bytes 3145736 | tf_op jit(solution)/shard_map/ppermute | solution.py:24
  100.1 4.8 %copy-start.1 = (f32[128,16,128]{0,2,1:T(8,128)S(1)}, f32[128,16,128]{0,2,1:T(8,128)}, u32[]{:S(2)}) copy-start(f32[128,16,128]{0,2,1:T(8,128)} %broadcast_multiply_fusion.2) | copy-start | bytes 3145732
  100.1 4.8 %copy-start.4 = (f32[1,1,128,2048]{2,3,1,0:T(8,128)S(1)}, f32[1,1,128,2048]{2,3,1,0:T(8,128)}, u32[]{:S(2)}) copy-start(f32[1,1,128,2048]{2,3,1,0:T(8,128)} %copy.53) | copy-start | bytes 3145732
  104.9 16.8 %copy-start.10 = (bf16[1,1,128,2048]{3,2,1,0:T(8,128)(2,1)S(1)}, bf16[1,1,128,2048]{3,2,1,0:T(8,128)(2,1)}, u32[]{:S(2)}) copy-start(bf16[1,1,128,2048]{3,2,1,0:T(8,128)(2,1)} %param.8) | copy-start | bytes 1572868
  107.5 16.9 %copy-start.6 = (f32[16,128,256]{2,1,0:T(8,128)S(1)}, f32[16,128,256]{2,1,0:T(8,128)}, u32[]{:S(2)}) copy-start(f32[16,128,256]{2,1,0:T(8,128)} %get-tuple-element.29) | copy-start | bytes 6291460
  127.8 1.2 copy-start.7
  127.8 1.5 copy-start.8
  130.0 1.2 copy-start.9
where the time goes:
time: 221 us; the launch traced here: 220 us
  blocking collectives  86.5 us (39%)
  waiting for transfers between devices  49.7 us (22%)
  starting transfers between devices  27.7 us (13%)
  matrix products  27.2 us (12%)
  other arithmetic  14.5 us (7%)
  local copies, waits for them, and re-layouts  14.3 us (6%)
    psum x1, blocking collectives, shards(): summed = lax.psum(totals.reshape(4, channels), ('dp', 'seq'))  86.5 us
    ppermute x3, waiting for transfers between devices, partner(): return lax.ppermute(block, axis, route)  35.5 us
    ppermute x3, starting transfers between devices, partner(): return lax.ppermute(block, axis, route)  16 us
    ppermute x1, waiting for transfers between devices, from_behind(): return lax.ppermute(block, axis, route)  14.2 us
    ppermute x1, starting transfers between devices, from_behind(): return lax.ppermute(block, axis, route)  11.7 us
    sub x2, matrix products, attend(): exped = jnp.exp(scores - jnp.max(scores, axis=-1, keepdims=True))  8.66 us
    dot_general x2, matrix products, attend(): jnp.einsum('thd,shd->hts', grad_out, val_mat, preferred_element_type=jnp....  5.55 us
  transfers between devices with their start and end apart: 4, of which 3 were waited for; matrix products, arithmetic and copies ran while one was open for 16% of the time, Pallas kernels for 0%

commit v1 on v0

--- a/solution.py
+++ b/solution.py
@@ -149,7 +149,7 @@
                 uppermost_result_derivative[step_index, 0].astype(jnp.float32),
                 received,
             )
-    summed = lax.psum(totals.reshape(4, channels), ("dp", "seq"))
+    summed = jnp.sum(lax.all_gather(totals.reshape(4, channels), ("dp", "seq")), axis=0)
     return summed[None]
 
 

time: 221 us -> 188 us (0.85)
  the two profiles are of different devices: /device:TPU:24 before, /device:TPU:56 now
where the time goes in v1:
time: 188 us; the launch traced here: 187 us
  blocking collectives  54.4 us (29%)
  waiting for transfers between devices  51 us (27%)
  matrix products  27.2 us (14%)
  starting transfers between devices  24.9 us (13%)
  other arithmetic  15.2 us (8%)
  local copies, waits for them, and re-layouts  14.3 us (8%)
    all_gather x1, blocking collectives, shards(): lax.all_gather(totals.reshape(4, channels), ('dp', 'seq'))  54.4 us
    ppermute x3, waiting for transfers between devices, partner(): return lax.ppermute(block, axis, route)  37.9 us
    ppermute x3, starting transfers between devices, partner(): return lax.ppermute(block, axis, route)  13.2 us
    ppermute x1, waiting for transfers between devices, from_behind(): return lax.ppermute(block, axis, route)  13.1 us
    ppermute x1, starting transfers between devices, from_behind(): return lax.ppermute(block, axis, route)  11.7 us
    sub x2, matrix products, attend(): exped = jnp.exp(scores - jnp.max(scores, axis=-1, keepdims=True))  8.66 us
    dot_general x2, matrix products, attend(): jnp.einsum('thd,shd->hts', grad_out, val_mat, preferred_element_type=jnp....  5.55 us
    dot_general x2, matrix products, shards(): jnp.einsum('hts,thd->shd', probs_low, grad_out, preferred_element_type=jn...  4 us
  transfers between devices with their start and end apart: 4, of which 3 were waited for; matrix products, arithmetic and copies ran while one was open for 18% of the time, Pallas kernels for 0%

profile of v1, /device:TPU:56, one launch (start us, length us, event | category | flops | bytes accessed | tf_op | source)
XLA Modules:
  0.0 187.2 jit_solution(14784241271362220789)
XLA Ops:
  0.0 2.7 %slice_convert_fusion = (f32[1,1,1,128,2048]{4,3,2,1,0:T(8,128)}, bf16[128,2048]{1,0:T(8,128)(2,1)}, bf16[128,2048]{1,0:T(8,128)(2,1)}, f32[1,1,1,128,2048]{4,3,2,1,0:T(8,128)S(1)}) fusion(bf16[1,2,1,128,2048]{4,3,2,1,0:T(8,128)(2,1)} %param.6), kind=kLoop, calls=%fused_computation.75 | loop fusion | flops 524288 | bytes 4194304 | tf_op jit(solution)/shard_map/convert_element_type | solution.py:28
  2.7 4.7 %collective-permute-start = (bf16[128,2048]{1,0:T(8,128)(2,1)}, bf16[128,2048]{1,0:T(8,128)(2,1)}, u32[]{:S(2)}, u32[]{:S(2)}) collective-permute-start(bf16[128,2048]{1,0:T(8,128)(2,1)} %get-tuple-element.12), channel_id=1, source_target_pairs={{0,1},{1,0},{2,3},{3,2},{4,5},{5,4},{6,7},{7,6},{8,9},{9,8},{10,11... | collective-permute-start | bytes 1572872 | tf_op jit(solution)/shard_map/ppermute | solution.py:18
  7.4 5.0 %collective-permute-start.1 = (bf16[128,2048]{1,0:T(8,128)(2,1)}, bf16[128,2048]{1,0:T(8,128)(2,1)}, u32[]{:S(2)}, u32[]{:S(2)}) collective-permute-start(bf16[128,2048]{1,0:T(8,128)(2,1)} %get-tuple-element.13), channel_id=1, source_target_pairs={{0,1},{1,0},{2,3},{3,2},{4,5},{5,4},{6,7},{7,6},{8,9},{9,8},{10,11... | collective-permute-start | bytes 1572872 | tf_op jit(solution)/shard_map/ppermute | solution.py:18
  12.6 0.2 or_reduce_fusion
  12.9 0.1 and_reduce_fusion.1
  13.0 0.6 gather_fusion
  13.7 0.3 copy.70
  14.1 0.1 broadcast_multiply_fusion.3
  14.2 0.6 copy-done.11
  14.8 1.5 copy.79
  16.5 0.1 and_reduce_fusion
  16.6 2.3 %copy.74 = f32[1,1,128,2048]{2,3,1,0:T(8,128)} copy(bf16[1,1,128,2048]{3,2,1,0:T(8,128)(2,1)} %param.7) | data formatting | bytes 1572864 | tf_op jit(solution)/shard_map/convert_element_type | solution.py:97
  18.9 0.6 gather_fusion.1
  19.5 1.1 broadcast_multiply_fusion.1
  20.6 13.8 %collective-permute-done = bf16[128,2048]{1,0:T(8,128)(2,1)} collective-permute-done((bf16[128,2048]{1,0:T(8,128)(2,1)}, bf16[128,2048]{1,0:T(8,128)(2,1)}, u32[]{:S(2)}, u32[]{:S(2)}) %collective-permute-start) | collective-permute-done | bytes 524320 | tf_op jit(solution)/shard_map/ppermute | solution.py:18
  34.4 1.2 copy.71
  35.8 1.1 broadcast_multiply_fusion.2
  36.9 3.9 %fusion.48 = (f32[16,128]{1,0:T(8,128)S(1)}, f32[16,128,256]{2,1,0:T(8,128)}) fusion(pred[256]{0:T(512)(128)(4,1)S(1)} %broadcast_bitcast_fusion.1, f32[16,128]{1,0:T(8,128)S(1)} %bitcast.123, f32[128,16,128]{0,2,1:T(8,128)} %broadcast_multiply_fusion.2, f32[128,16,128]{0,2,1:T(8,128)S(1)} %broadcast_multiply_fusion.3, f32[16,128]{1,0:T(8,128)S(1)} %bitcast.118), kind=kOutput, calls=%fused_computation.118 | convolution fusion | flops 138412288 | bytes 4219136 | tf_op jit(solution)/shard_map/sub | solution.py:66
  40.8 2.8 %fusion.26 = f32[16,128,256]{2,1,0:T(8,128)S(1)} fusion(f32[128,16,128]{0,2,1:T(8,128)} %bitcast.109, f32[16,128]{1,0:T(8,128)S(1)} %bitcast.140, f32[16,128,256]{2,1,0:T(8,128)} %get-tuple-element.24, f32[16,128]{1,0:T(8,128)S(1)} %get-tuple-element.23), kind=kOutput, calls=%fused_computation.70 | convolution fusion | flops 135790592 | bytes 5259264 | tf_op jit(solution)/shard_map/hts,thd->shd/dot_general | solution.py:121
  43.6 0.3 copy-done.5
  43.9 2.2 %multiply_reduce_fusion.1 = (f32[16,128]{1,0:T(8,128)S(1)}, f32[16,128,256]{2,1,0:T(8,128)S(1)}) fusion(f32[16,128,256]{2,1,0:T(8,128)S(1)} %copy-done.5, f32[16,128]{1,0:T(8,128)S(1)} %get-tuple-element.23, f32[16,128]{1,0:T(8,128)S(1)} %bitcast.130, f32[128,16,128]{0,2,1:T(8,128)S(1)} %copy-done, f32[128,16,128]{0,2,1:T(8,128)S(1)} %broadcast_multiply_fusion.3, ...), kind=kOutput, calls=%fused_computation.23 | convolution fusion | flops 137885696 | bytes 7372800 | tf_op jit(solution)/shard_map/thd,shd->hts/dot_general | solution.py:71
  46.1 0.7 multiply_convert_fusion.3
  46.9 1.9 %fusion.5 = (f32[16,128]{1,0:T(8,128)S(1)}, f32[16,128]{1,0:T(8,128)S(1)}, f32[256,16,128]{0,2,1:T(8,128)S(1)}) fusion(f32[128,16,128]{0,2,1:T(8,128)S(1)} %copy-done, f32[128,16,128]{0,2,1:T(8,128)S(1)} %broadcast_multiply_fusion.3, f32[16,128,256]{2,1,0:T(8,128)S(1)} %fusion.26, f32[16,128]{1,0:T(8,128)S(1)} %bitcast.131, ...), kind=kOutput, calls=%fused_computation.15 | convolution fusion | flops 139456512 | bytes 7380992 | tf_op jit(solution)/shard_map/hts,thd->shd/dot_general | solution.py:118
  48.8 1.9 %multiply_reduce_fusion.3 = (f32[128,16]{0,1:T(8,128)S(1)}, f32[128,16]{0,1:T(8,128)S(1)}, f32[16,128]{1,0:T(8,128)S(1)}, f32[16,128,128]{2,1,0:T(8,128)}) fusion(f32[128,16,128]{0,2,1:T(8,128)S(1)} %broadcast_multiply_fusion.3, f32[256,16,128]{0,2,1:T(8,128)S(1)} %get-tuple-element.10, f32[16,128]{1,0:T(8,128)S(1)} %broadcast_multiply_fusion.5, ...), kind=kOutput, calls=%fused_computation.48 | convolution fusion | flops 138143744 | bytes 8429568 | tf_op jit(solution)/shard_map/hts,shd->thd/dot_general | solution.py:114
  50.8 1.0 multiply_convert_fusion.7
  51.8 3.5 %collective-permute-start.2 = (bf16[128,16,128]{0,2,1:T(8,128)(2,1)}, bf16[128,16,128]{0,2,1:T(8,128)(2,1)}, u32[]{:S(2)}, u32[]{:S(2)}) collective-permute-start(bf16[128,16,128]{0,2,1:T(8,128)(2,1)} %multiply_convert_fusion.7), channel_id=1, source_target_pairs={{0,1},{1,0},{2,3},{3,2},{4,5},{5,4},{6,7},{7,6},{8,9},{9,8},{10,11... | collective-permute-start | bytes 1572872 | tf_op jit(solution)/shard_map/ppermute | solution.py:18
  55.3 1.2 copy.80
  56.7 24.1 %collective-permute-done.2 = bf16[128,16,128]{0,2,1:T(8,128)(2,1)} collective-permute-done((bf16[128,16,128]{0,2,1:T(8,128)(2,1)}, bf16[128,16,128]{0,2,1:T(8,128)(2,1)}, u32[]{:S(2)}, u32[]{:S(2)}) %collective-permute-start.2) | collective-permute-done | bytes 524320 | tf_op jit(solution)/shard_map/ppermute | solution.py:18
  80.7 3.6 %convert_add_fusion = f32[128,16,128]{0,2,1:T(8,128)} fusion(bf16[128,16,128]{0,2,1:T(8,128)(2,1)} %collective-permute-done.2, f32[128,16,128]{0,2,1:T(8,128)} %bitcast.110, f32[128,16]{0,1:T(8,128)S(1)} %broadcast_multiply_fusion.7, f32[128,16]{0,1:T(8,128)S(1)} %add_rsqrt_fusion.3, f32[256,16,128]{0,2,1:T(8,128)} %copy-done.2, ...), kind=kLoop, calls=%fused_computation.45 | loop fusion | flops 2359296 | bytes 5791744 | tf_op jit(solution)/shard_map/add | solution.py:142
  84.3 2.6 %copy.83 = f32[128,2048]{1,0:T(8,128)} copy(f32[128,2048]{0,1:T(8,128)} %bitcast.113) | data formatting | bytes 2097152 | tf_op jit(solution)/shard_map/reshape | solution.py:146
  86.9 11.7 %collective-permute-start.3 = (f32[128,2048]{1,0:T(8,128)}, f32[128,2048]{1,0:T(8,128)}, u32[]{:S(2)}, u32[]{:S(2)}) collective-permute-start(f32[128,2048]{1,0:T(8,128)} %copy.83), channel_id=1, source_target_pairs={{16,0},{32,16},{48,32},{64,48},{80,64},{96,80},{112,96},{128,112},... | collective-permute-start | bytes 3145736 | tf_op jit(solution)/shard_map/ppermute | solution.py:24
  98.6 1.1 broadcast_multiply_fusion
  99.7 4.8 %fusion.49 = (f32[16,128]{1,0:T(8,128)S(1)}, f32[16,128,256]{2,1,0:T(8,128)}) fusion(pred[256]{0:T(512)(128)(4,1)S(1)} %broadcast_bitcast_fusion, f32[16,128]{1,0:T(8,128)S(1)} %bitcast.125, f32[128,16,128]{0,2,1:T(8,128)} %broadcast_multiply_fusion, f32[128,16,128]{0,2,1:T(8,128)} %broadcast_multiply_fusion.1, f32[16,128]{1,0:T(8,128)S(1)} %bitcast.120), kind=kOutput, calls=%fused_computation.119 | convolution fusion | flops 138412288 | bytes 4219136 | tf_op jit(solution)/shard_map/sub | solution.py:66
  104.5 2.6 %fusion.12 = f32[16,128]{1,0:T(8,128)S(1)} fusion(f32[128,16,128]{0,2,1:T(8,128)S(1)} %bitcast.112, f32[16,128]{1,0:T(8,128)S(1)} %bitcast.132, f32[128,16,128]{0,2,1:T(8,128)S(1)} %copy-done.1, f32[128,16,128]{0,2,1:T(8,128)S(1)} %broadcast_multiply_fusion.3, f32[16,128,256]{2,1,0:T(8,128)} %get-tuple-element.24, f32[16,128]{1,0:T(8,128)S(1)} %get-tuple-element.23), kind=kOutput, calls=%fused_computation.37 | convolution fusion | flops 137361408 | bytes 5267456 | tf_op jit(solution)/shard_map/hts,shd->thd/dot_general | solution.py:69
  107.1 13.1 %collective-permute-done.3 = f32[128,2048]{1,0:T(8,128)} collective-permute-done((f32[128,2048]{1,0:T(8,128)}, f32[128,2048]{1,0:T(8,128)}, u32[]{:S(2)}, u32[]{:S(2)}) %collective-permute-start.3) | collective-permute-done | bytes 1048608 | tf_op jit(solution)/shard_map/ppermute | solution.py:24
  120.2 1.3 convert_select_fusion
  121.5 1.3 copy.84
  122.9 3.4 %multiply_reduce_fusion = (f32[16,128]{1,0:T(8,128)S(1)}, f32[16,128,256]{2,1,0:T(8,128)S(1)}) fusion(f32[16,128,256]{2,1,0:T(8,128)S(1)} %copy-done.6, f32[16,128]{1,0:T(8,128)S(1)} %get-tuple-element.28, f32[16,128]{1,0:T(8,128)S(1)} %bitcast.133, f32[128,16,128]{0,2,1:T(8,128)} %broadcast_multiply_fusion, f32[128,16,128]{0,2,1:T(8,128)} %broadcast_multiply_fusion.1, ...), kind=kOutput, calls=%fused_computation.17 | convolution fusion | flops 137885696 | bytes 7372800 | tf_op jit(solution)/shard_map/thd,shd->hts/dot_general | solution.py:71
  126.2 0.8 multiply_convert_fusion
  127.0 0.4 copy-done.7
  127.5 0.3 copy-done.8
  127.8 0.7 fusion.13
  128.5 0.7 fusion.3
  129.2 0.5 copy-done.9
  129.7 1.1 fusion.2
  130.8 1.2 fusion.14
  132.1 54.4 %all_gather.3 = f32[16,4,2048]{2,1,0:T(4,128)S(1)} all-gather(f32[1,4,2048]{2,1,0:T(4,128)S(1)} %maximum_add_fusion), channel_id=1, replica_groups=mesh['segment'=32,'dp'=8,'seq'=2] {'dp','seq'}, dimensions={0}, use_global_device_ids=true | all-gather | bytes 557056 | tf_op jit(solution)/shard_map/all_gather | solution.py:152
  186.5 0.7 reduce_sum.189
  (45 shorter events, 0.8 us)
Async XLA Ops:
  0.0 12.8 %copy-start.13 = (s32[1,2,1,2]{3,2,1,0:T(1,128)S(1)}, s32[1,2,1,2]{3,2,1,0:T(1,128)}, u32[]{:S(2)}) copy-start(s32[1,2,1,2]{3,2,1,0:T(1,128)} %param.11) | copy-start | bytes 52
  0.0 12.8 %copy-start.12 = (s32[1,2,1,2,2]{4,3,2,1,0:T(2,128)S(1)}, s32[1,2,1,2,2]{4,3,2,1,0:T(2,128)}, u32[]{:S(2)}) copy-start(s32[1,2,1,2,2]{4,3,2,1,0:T(2,128)} %param.10) | copy-start | bytes 100
  2.7 31.7 %collective-permute-start = (bf16[128,2048]{1,0:T(8,128)(2,1)}, bf16[128,2048]{1,0:T(8,128)(2,1)}, u32[]{:S(2)}, u32[]{:S(2)}) collective-permute-start(bf16[128,2048]{1,0:T(8,128)(2,1)} %get-tuple-element.12), channel_id=1, source_target_pairs={{0,1},{1,0},{2,3},{3,2},{4,5},{5,4},{6,7},{7,6},{8,9},{9,8},{10,11... | collective-permute-start | bytes 1572872 | tf_op jit(solution)/shard_map/ppermute | solution.py:18
  7.4 47.9 %collective-permute-start.1 = (bf16[128,2048]{1,0:T(8,128)(2,1)}, bf16[128,2048]{1,0:T(8,128)(2,1)}, u32[]{:S(2)}, u32[]{:S(2)}) collective-permute-start(bf16[128,2048]{1,0:T(8,128)(2,1)} %get-tuple-element.13), channel_id=1, source_target_pairs={{0,1},{1,0},{2,3},{3,2},{4,5},{5,4},{6,7},{7,6},{8,9},{9,8},{10,11... | collective-permute-start | bytes 1572872 | tf_op jit(solution)/shard_map/ppermute | solution.py:18
  14.0 0.8 copy-start.11
  40.8 2.9 %copy-start = (f32[128,16,128]{0,2,1:T(8,128)S(1)}, f32[128,16,128]{0,2,1:T(8,128)}, u32[]{:S(2)}) copy-start(f32[128,16,128]{0,2,1:T(8,128)} %broadcast_multiply_fusion.2) | copy-start | bytes 3145732
  40.8 2.9 %copy-start.3 = (f32[1,1,128,2048]{2,3,1,0:T(8,128)S(1)}, f32[1,1,128,2048]{2,3,1,0:T(8,128)}, u32[]{:S(2)}) copy-start(f32[1,1,128,2048]{2,3,1,0:T(8,128)} %copy.74) | copy-start | bytes 3145732
  40.8 3.2 %copy-start.5 = (f32[16,128,256]{2,1,0:T(8,128)S(1)}, f32[16,128,256]{2,1,0:T(8,128)}, u32[]{:S(2)}) copy-start(f32[16,128,256]{2,1,0:T(8,128)} %get-tuple-element.24) | copy-start | bytes 6291460
  48.8 1.9 %copy-start.2 = (f32[256,16,128]{0,2,1:T(8,128)}, f32[256,16,128]{0,2,1:T(8,128)S(1)}, u32[]{:S(2)}) copy-start(f32[256,16,128]{0,2,1:T(8,128)S(1)} %get-tuple-element.10) | copy-start | bytes 6291460
  51.8 29.0 %collective-permute-start.2 = (bf16[128,16,128]{0,2,1:T(8,128)(2,1)}, bf16[128,16,128]{0,2,1:T(8,128)(2,1)}, u32[]{:S(2)}, u32[]{:S(2)}) collective-permute-start(bf16[128,16,128]{0,2,1:T(8,128)(2,1)} %multiply_convert_fusion.7), channel_id=1, source_target_pairs={{0,1},{1,0},{2,3},{3,2},{4,5},{5,4},{6,7},{7,6},{8,9},{9,8},{10,11... | collective-permute-start | bytes 1572872 | tf_op jit(solution)/shard_map/ppermute | solution.py:18
  86.9 33.2 %collective-permute-start.3 = (f32[128,2048]{1,0:T(8,128)}, f32[128,2048]{1,0:T(8,128)}, u32[]{:S(2)}, u32[]{:S(2)}) collective-permute-start(f32[128,2048]{1,0:T(8,128)} %copy.83), channel_id=1, source_target_pairs={{16,0},{32,16},{48,32},{64,48},{80,64},{96,80},{112,96},{128,112},... | collective-permute-start | bytes 3145736 | tf_op jit(solution)/shard_map/ppermute | solution.py:24
  99.7 4.8 %copy-start.1 = (f32[128,16,128]{0,2,1:T(8,128)S(1)}, f32[128,16,128]{0,2,1:T(8,128)}, u32[]{:S(2)}) copy-start(f32[128,16,128]{0,2,1:T(8,128)} %broadcast_multiply_fusion.2) | copy-start | bytes 3145732
  99.7 4.8 %copy-start.4 = (f32[1,1,128,2048]{2,3,1,0:T(8,128)S(1)}, f32[1,1,128,2048]{2,3,1,0:T(8,128)}, u32[]{:S(2)}) copy-start(f32[1,1,128,2048]{2,3,1,0:T(8,128)} %copy.74) | copy-start | bytes 3145732
  104.5 15.7 %copy-start.10 = (bf16[1,1,128,2048]{3,2,1,0:T(8,128)(2,1)S(1)}, bf16[1,1,128,2048]{3,2,1,0:T(8,128)(2,1)}, u32[]{:S(2)}) copy-start(bf16[1,1,128,2048]{3,2,1,0:T(8,128)(2,1)} %param.8) | copy-start | bytes 1572868
  107.1 15.8 %copy-start.6 = (f32[16,128,256]{2,1,0:T(8,128)S(1)}, f32[16,128,256]{2,1,0:T(8,128)}, u32[]{:S(2)}) copy-start(f32[16,128,256]{2,1,0:T(8,128)} %get-tuple-element.29) | copy-start | bytes 6291460
  126.2 1.2 copy-start.7
  126.2 1.5 copy-start.8
  128.5 1.2 copy-start.9
